TPU v7x, 128 devices: a whole 4x4x4 slice. The times are simulated.
128 devices in a mesh: gx: 16 (over x, z_lo, core), gy: 8 (over z_hi, y).
Axes of the slice: x: 4, y: 4, z: 4 (z_hi: 2, z_lo: 2; z = z_hi * 2 + z_lo), core: 2. Of those that a mesh axis runs over, the one named last changes fastest.
Arguments:
- fields: float32 [5, 256, 256, 128], P(None, 'gx', 'gy'), may hold values from -6 to 6
- patch_weight: bfloat16 [2560, 512], replicated, may hold values from -0.125 to 0.125
- trainer_of: int32 [8192, 1], P(('gx', 'gy')), may hold values from 0 to 127; in each aligned block of 64 rows (0 to 63, 64 to 127, ...) at most 2 rows name the same one
- lag_index: int32 [32, 32, 16], P('gx', 'gy'), may hold values from 0 to 1
- w_in: bfloat16 [128, 512, 2048], P(('gx', 'gy')), may hold values from -0.25 to 0.25
- b_in: float32 [128, 2048], P(('gx', 'gy')), may hold values from -3 to 3
- w_out: bfloat16 [128, 2048, 512], P(('gx', 'gy')), may hold values from -0.125 to 0.125
- b_out: float32 [128, 512], P(('gx', 'gy')), may hold values from -3 to 3
Outputs:
- new_fields: float32 [5, 256, 256, 128], P(None, 'gx', 'gy')
- patch_gradient: float32 [2560, 512], replicated
- w_in_gradient: float32 [128, 512, 2048], P(('gx', 'gy'))
- b_in_gradient: float32 [128, 2048], P(('gx', 'gy'))
- w_out_gradient: float32 [128, 2048, 512], P(('gx', 'gy'))
- b_out_gradient: float32 [128, 512], P(('gx', 'gy'))
Inputs may be any that keep to these rules, and one draw needn't show every extreme that they name: `trainer_of`: among the 64 rows of one brick, no trainer is named more than 2 times.
All inputs are finite; a program needn't handle non-finite values.
Results may differ from a plain program's by a relative error of at most 0.0062.
Values may be sent and summed in bfloat16 or wider, within the bound.
No kernel may reach another device: no remote copies, remote signals or barrier semaphores. Data moves between devices by JAX's collectives and lax.ppermute only.
A program may use at most 128 MiB of HBM per device.

v0:
```python
import jax
import jax.numpy as jnp
from jax import lax
from jax.sharding import PartitionSpec as P

FIELDS = 5
PATCH = 8
STEPS = 3
EMBED = 512
BLOCK_ROWS = 2
time_step = 0.2
viscosity = 0.5
drift_x = 0.6
drift_y = -0.4
drift_z = 0.3
error_weight = 0.0625


def with_halo(x, sides, width):
    edges = {}
    for axis, dim in sides:
        count, length = (lax.axis_size(axis), x.shape[dim])
        up = [(i, (i + 1) % count) for i in range(count - 1)]
        last = lax.slice_in_dim(x, length - width, length, axis=dim)
        initial = lax.slice_in_dim(x, 0, width, axis=dim)
        edges[dim] = (
            lax.ppermute(last, axis, up),
            lax.ppermute(initial, axis, [(b, a) for a, b in up]),
        )
    done = []
    for _, dim in sides:
        low, high = edges[dim]
        around = [(width, width) if d in done else (0, 0) for d in range(x.ndim)]
        x = jnp.concatenate([jnp.pad(low, around), x, jnp.pad(high, around)], axis=dim)
        done.append(dim)
    return x


def sent_together(arrays, axis, split_dim, concat_dim, along):
    columns = [a.reshape(*a.shape[:along], -1) for a in arrays]
    both = jnp.concatenate(columns, axis=along)
    result, at, finished = (
        lax.all_to_all(both, axis, split_axis=split_dim, concat_axis=concat_dim, tiled=True),
        0,
        [],
    )
    for a, column in zip(arrays, columns):
        piece = result[..., at : at + column.shape[along]]
        finished.append(piece.reshape(*piece.shape[:along], *a.shape[along:]))
        at += column.shape[along]
    return tuple(finished)


def shifted(padded, dimension, offset):
    window = [slice(None)]
    for other in (1, 2, 3):
        window.append(slice(2, padded.shape[other] - 2))
    window[dimension] = slice(2 + offset, padded.shape[dimension] - 2 + offset)
    return padded[tuple(window)]


def tendency(padded):
    gradients = []
    laplacian = 0.0
    for dimension in (1, 2, 3):
        back_two = shifted(padded, dimension, -2)
        back_one = shifted(padded, dimension, -1)
        middle = shifted(padded, dimension, 0)
        ahead_one = shifted(padded, dimension, 1)
        ahead_two = shifted(padded, dimension, 2)
        gradients.append((back_two - 8.0 * back_one + 8.0 * ahead_one - ahead_two) / 12.0)
        laplacian = (
            laplacian
            + (-back_two + 16.0 * back_one - 30.0 * middle + 16.0 * ahead_one - ahead_two) / 12.0
        )
    carried = drift_x * gradients[0] + drift_y * gradients[1] + drift_z * gradients[2]
    divergence = gradients[0][1] + gradients[1][2] + gradients[2][3]
    acoustic = jnp.stack(
        [divergence, gradients[0][4], gradients[1][4], gradients[2][4], divergence]
    )
    return viscosity * laplacian - carried - acoustic


def contract_rows(left, right):
    return lax.dot_general(
        left, right, (((0,), (0,)), ((), ())), preferred_element_type=jnp.float32
    )


def contract_cols(left, right):
    return lax.dot_general(
        left, right, (((1,), (1,)), ((), ())), preferred_element_type=jnp.float32
    )


def trainer_step(source, target, valid, w_first, b_first, w_second, b_second):
    pre = jnp.dot(source, w_first, preferred_element_type=jnp.float32) + b_first
    hidden = jax.nn.silu(pre).astype(jnp.bfloat16)
    predict = jnp.dot(hidden, w_second, preferred_element_type=jnp.float32) + b_second
    error = (error_weight * (predict - target.astype(jnp.float32)) * valid).astype(jnp.bfloat16)
    b_second_grad = jnp.sum(error.astype(jnp.float32), axis=0)
    w_second_grad = contract_rows(hidden, error)
    back = contract_cols(error, w_second)
    sigma = jax.nn.sigmoid(pre)
    pre_grad = (back * sigma * (1.0 + pre * (1.0 - sigma))).astype(jnp.bfloat16)
    b_first_grad = jnp.sum(pre_grad.astype(jnp.float32), axis=0)
    w_first_grad = contract_rows(source, pre_grad)
    source_grad = contract_cols(pre_grad, w_first).astype(jnp.bfloat16)
    return (source_grad, w_first_grad, b_first_grad, w_second_grad, b_second_grad)


def patchify(state):
    width_x, width_y, width_z = (state.shape[1], state.shape[2], state.shape[3])
    shaped = state.reshape(
        FIELDS, width_x // PATCH, PATCH, width_y // PATCH, PATCH, width_z // PATCH, PATCH
    )
    return shaped.transpose(1, 3, 5, 0, 2, 4, 6).reshape(-1, FIELDS * PATCH**3)


def pad_third(current):
    return jnp.pad(current, ((0, 0), (0, 0), (0, 0), (2, 2)))


def advance(fields):
    states = []
    current = fields
    for counter in range(STEPS):
        padded = with_halo(current, (("gx", 1), ("gy", 2)), 2)
        current = current + time_step * tendency(pad_third(padded))
        states.append(current)
    return states


def per_device(fields, patch_weight, trainer_of, lag_index, w_in, b_in, w_out, b_out):
    states = advance(fields)
    devices = lax.axis_size("gx") * lax.axis_size("gy")
    lag_rows = lag_index.reshape(-1, 1)
    picked = patchify(states[0].astype(jnp.bfloat16))
    picked = jnp.where(lag_rows == 1, patchify(states[1].astype(jnp.bfloat16)), picked)
    target = jnp.dot(
        patchify(states[-1].astype(jnp.bfloat16)), patch_weight, preferred_element_type=jnp.float32
    ).astype(jnp.bfloat16)
    patch_count = picked.shape[0]
    block_count = patch_count // BLOCK_ROWS
    slot_count = max(2, 2 * block_count // devices)
    owners = trainer_of[:, 0]
    onehot = (owners[:, None] == jnp.arange(devices, dtype=jnp.int32)[None, :]).astype(jnp.int32)
    within_rank = jnp.sum((jnp.cumsum(onehot, axis=0) - onehot) * onehot, axis=1)
    block_slot = owners * slot_count + within_rank

    def into_slots(rows):
        width = rows.shape[1]
        blocks = rows.reshape(block_count, BLOCK_ROWS, width)
        buffer = (
            jnp.zeros((devices * slot_count, BLOCK_ROWS, width), rows.dtype)
            .at[block_slot]
            .set(blocks)
        )
        return buffer.reshape(devices, slot_count, BLOCK_ROWS, width)

    valid_send = jnp.zeros((devices * slot_count,), jnp.bfloat16).at[block_slot].set(1.0)
    valid_send = valid_send.reshape(devices, slot_count)
    source = jnp.dot(picked, patch_weight, preferred_element_type=jnp.float32).astype(jnp.bfloat16)
    got_source, got_target, got_valid = sent_together(
        (into_slots(source), into_slots(target), valid_send), ("gx", "gy"), 0, 0, 2
    )
    valid_rows = jnp.repeat(got_valid.astype(jnp.float32).reshape(-1), BLOCK_ROWS)[:, None]
    results = trainer_step(
        got_source.reshape(-1, EMBED),
        got_target.reshape(-1, EMBED),
        valid_rows,
        w_in[0],
        b_in[0],
        w_out[0],
        b_out[0],
    )
    returned = lax.all_to_all(
        results[0].reshape(devices, slot_count, BLOCK_ROWS, EMBED),
        ("gx", "gy"),
        split_axis=0,
        concat_axis=0,
        tiled=True,
    )
    source_grad = returned.reshape(devices * slot_count, BLOCK_ROWS, EMBED)[block_slot]
    partial_value = contract_rows(picked, source_grad.reshape(patch_count, EMBED))
    patch_gradient = lax.psum(partial_value, ("gx", "gy"))
    return (
        states[-1],
        patch_gradient,
        results[1][None],
        results[2][None],
        results[3][None],
        results[4][None],
    )


def solution(mesh):
    in_specs = (
        P(None, "gx", "gy", None),
        P(),
        P(("gx", "gy"), None),
        P("gx", "gy", None),
        P(("gx", "gy"), None, None),
        P(("gx", "gy"), None),
        P(("gx", "gy"), None, None),
        P(("gx", "gy"), None),
    )
    out_specs = (
        P(None, "gx", "gy", None),
        P(),
        P(("gx", "gy"), None, None),
        P(("gx", "gy"), None),
        P(("gx", "gy"), None, None),
        P(("gx", "gy"), None),
    )
    return jax.shard_map(
        per_device, mesh=mesh, in_specs=in_specs, out_specs=out_specs, check_vma=False
    )
```

profile of v0, /device:TPU:1, one launch (start us, length us, event | category | flops | bytes accessed | tf_op | source)
XLA Modules:
  0.0 482.5 jit_solution(16049055990114909716)
XLA Ops:
  7.2 1.3 fusion.63
  8.5 4.7 collective-permute-start.2
  15.5 2.9 collective-permute-start.1
  18.3 3.4 collective-permute-start
  26.1 1.8 constant_dynamic-update-slice_fusion
  27.9 1.6 select_maximum_fusion.8
  29.5 2.3 broadcast_multiply_fusion.2
  33.7 4.0 fusion.57
  38.8 4.9 %collective-permute-start.6 = (f32[5,16,2,128]{3,2,1,0:T(2,128)S(1)}, f32[5,16,2,128]{3,2,1,0:T(2,128)}, u32[]{:S(2)}, u32[]{:S(2)}) collective-permute-start(f32[5,16,2,128]{3,2,1,0:T(2,128)S(1)} %get-tuple-element.34), channel_id=1, source_target_pairs={{0,1},{1,2},{2,3},{3,4},{4,5},{5,6},{6,7},{8,9},{9,10},{10,11},{11... | collective-permute-start | bytes 245768 | tf_op jit(solution)/shard_map/ppermute | solution.py:27
  45.0 2.8 collective-permute-start.4
  47.8 1.9 collective-permute-start.5
  49.9 1.5 scatter_custom_fusion.2
  51.6 14.5 %reshape.74 = bf16[5,2,8,4,8,16,8]{6,5,4,3,2,1,0:T(8,128)(2,1)} reshape(bf16[5,16,32,128]{3,2,1,0:T(8,128)(2,1)} %get-tuple-element.10) | data formatting | bytes 1310720 | tf_op jit(solution)/shard_map/reshape | solution.py:114
  66.1 13.3 %copy.21 = bf16[2,4,16,5,8,8,8]{2,1,0,6,5,4,3:T(4,128)(2,1)} copy(bf16[2,4,16,5,8,8,8]{6,2,5,1,4,0,3:T(8,128)(2,1)} %bitcast.73) | data formatting | bytes 1310720 | tf_op jit(solution)/shard_map/transpose | solution.py:117
  79.4 8.1 %reshape.76 = bf16[128,2560]{0,1:T(8,128)(2,1)} reshape(bf16[2,4,16,5,8,8,8]{2,1,0,6,5,4,3:T(4,128)(2,1)} %copy.21) | data formatting | bytes 1310720 | tf_op jit(solution)/shard_map/reshape | solution.py:117
  89.4 4.6 select_maximum_fusion.4
  96.7 3.9 fusion.55
  102.4 4.9 %collective-permute-start.10 = (f32[5,16,2,128]{3,2,1,0:T(2,128)}, f32[5,16,2,128]{3,2,1,0:T(2,128)}, u32[]{:S(2)}, u32[]{:S(2)}) collective-permute-start(f32[5,16,2,128]{3,2,1,0:T(2,128)} %get-tuple-element.30), channel_id=1, source_target_pairs={{0,1},{1,2},{2,3},{3,4},{4,5},{5,6},{6,7},{8,9},{9,10},{10,11},{11... | collective-permute-start | bytes 245768 | tf_op jit(solution)/shard_map/ppermute | solution.py:27
  108.6 3.9 collective-permute-start.8
  112.5 2.1 collective-permute-start.9
  114.6 14.4 %reshape.73 = bf16[5,2,8,4,8,16,8]{6,5,4,3,2,1,0:T(8,128)(2,1)} reshape(bf16[5,16,32,128]{3,2,1,0:T(8,128)(2,1)} %get-tuple-element.8) | data formatting | bytes 1310720 | tf_op jit(solution)/shard_map/reshape | solution.py:114
  129.1 13.3 %copy.20 = bf16[2,4,16,5,8,8,8]{2,1,0,6,5,4,3:T(4,128)(2,1)} copy(bf16[2,4,16,5,8,8,8]{6,2,5,1,4,0,3:T(8,128)(2,1)} %bitcast.74) | data formatting | bytes 1310720 | tf_op jit(solution)/shard_map/transpose | solution.py:117
  142.4 8.1 %reshape.75 = bf16[128,2560]{0,1:T(8,128)(2,1)} reshape(bf16[2,4,16,5,8,8,8]{2,1,0,6,5,4,3:T(4,128)(2,1)} %copy.20) | data formatting | bytes 1310720 | tf_op jit(solution)/shard_map/reshape | solution.py:117
  150.5 1.8 convolution_convert_fusion.1
  153.3 5.4 %scatter_fusion = bf16[256,2,512]{2,1,0:T(2,128)(2,1)S(1)} fusion(bf16[256,2,512]{2,1,0:T(2,128)(2,1)S(1)} %broadcast.110.clone.1, s32[64]{0:T(128)S(1)} %fusion.50, bf16[64,2,512]{2,1,0:T(2,128)(2,1)} %reshape.97), kind=kCustom, calls=%fused_computation.1 | custom fusion | bytes 393472 | tf_op jit(solution)/shard_map/scatter | solution.py:157
  161.7 4.6 select_maximum_fusion
  169.0 4.1 fusion.53
  173.1 14.4 %reshape.78 = bf16[5,2,8,4,8,16,8]{6,5,4,3,2,1,0:T(8,128)(2,1)} reshape(bf16[5,16,32,128]{3,2,1,0:T(8,128)(2,1)} %get-tuple-element.6) | data formatting | bytes 1310720 | tf_op jit(solution)/shard_map/reshape | solution.py:114
  187.6 13.3 %copy.22 = bf16[2,4,16,5,8,8,8]{2,1,0,6,5,4,3:T(4,128)(2,1)} copy(bf16[2,4,16,5,8,8,8]{6,2,5,1,4,0,3:T(8,128)(2,1)} %bitcast.75) | data formatting | bytes 1310720 | tf_op jit(solution)/shard_map/transpose | solution.py:117
  200.9 7.5 %reshape.79 = bf16[128,2560]{0,1:T(8,128)(2,1)S(1)} reshape(bf16[2,4,16,5,8,8,8]{2,1,0,6,5,4,3:T(4,128)(2,1)} %copy.22) | data formatting | bytes 1310720 | tf_op jit(solution)/shard_map/reshape | solution.py:117
  209.3 2.5 scatter_fusion.1
  212.2 1.9 pad_maximum_fusion.8
  214.0 20.5 %all-to-all-start = ((bf16[128,2,2049]{2,1,0:T(2,128)(2,1)}), bf16[128,2,2049]{2,1,0:T(2,128)(2,1)S(1)}, u32[]{:S(2)}, u32[]{:S(2)}) async-start(bf16[128,2,2049]{2,1,0:T(2,128)(2,1)} %pad_maximum_fusion.8), calls=%async_computation | async-start | bytes 2228224 | tf_op jit(solution)/shard_map/all_to_all | solution.py:43
  234.5 19.8 %all-to-all-done = bf16[128,2,2049]{2,1,0:T(2,128)(2,1)S(1)} async-done(((bf16[128,2,2049]{2,1,0:T(2,128)(2,1)}), bf16[128,2,2049]{2,1,0:T(2,128)(2,1)S(1)}, u32[]{:S(2)}, u32[]{:S(2)}) %all-to-all-start) | async-done | bytes 1049120 | tf_op jit(solution)/shard_map/all_to_all | solution.py:43
  255.6 1.8 reshape.84
  257.8 3.0 fusion.6
  260.9 1.9 convert_reduce_fusion.1
  262.9 3.0 convert_reduce_fusion
  265.9 1.4 copy-done.11
  269.5 5.0 %all-to-all-start.1 = ((bf16[128,2,2,512]{3,2,1,0:T(2,128)(2,1)}), bf16[128,2,2,512]{3,2,1,0:T(2,128)(2,1)S(1)}, u32[]{:S(2)}, u32[]{:S(2)}) async-start(bf16[128,2,2,512]{3,2,1,0:T(2,128)(2,1)} %reshape.81), calls=%async_computation.1 | async-start | bytes 1048576 | tf_op jit(solution)/shard_map/all_to_all | solution.py:177
  274.6 12.3 %broadcast_select_fusion = bf16[2,4,16,5,8,8,8]{6,2,5,1,4,0,3:T(8,128)(2,1)} fusion(pred[2,4,16]{2,1,0:T(4,128)(4,1)S(1)} %broadcast_compare_fusion, bf16[5,2,8,4,8,16,8]{6,5,4,3,2,1,0:T(8,128)(2,1)} %reshape.74, bf16[5,2,8,4,8,16,8]{6,5,4,3,2,1,0:T(8,128)(2,1)} %reshape.73), kind=kLoop, calls=%fused_computation.4 | loop fusion | flops 327680 | bytes 1966208 | tf_op jit(solution)/shard_map/jit(_where)/select_n | solution.py:139
  286.9 13.3 %copy.19 = bf16[2,4,16,5,8,8,8]{2,1,0,6,5,4,3:T(4,128)(2,1)} copy(bf16[2,4,16,5,8,8,8]{6,2,5,1,4,0,3:T(8,128)(2,1)} %broadcast_select_fusion) | data formatting | bytes 1310720 | tf_op jit(solution)/shard_map/jit(_where)/select_n | solution.py:139
  300.2 7.3 %select_n.17 = bf16[128,2560]{0,1:T(8,128)(2,1)S(1)} reshape(bf16[2,4,16,5,8,8,8]{2,1,0,6,5,4,3:T(4,128)(2,1)} %copy.19) | data formatting | bytes 1310720 | tf_op jit(solution)/shard_map/jit(_where)/select_n | solution.py:139
  308.5 3.2 fusion.65
  311.7 5.0 %convolution_bitcast_fusion.1 = f32[1,512,2048]{2,1,0:T(8,128)} fusion(bf16[512,512]{1,0:T(8,128)(2,1)S(1)} %reshape_reshape.16, bf16[512,2048]{1,0:T(8,128)(2,1)} %copy-done.11), kind=kOutput, calls=%fused_computation.23 | convolution fusion | flops 1073741824 | bytes 6815744 | tf_op jit(solution)/shard_map/dot_general | solution.py:85
  316.7 3.5 convolution_bitcast_fusion
  320.2 149.4 %all-reduce.11.cloned.1.call-done = f32[2560,512]{1,0:T(8,128)} async-done(((f32[2560,512]{1,0:T(8,128)}), f32[2560,512]{1,0:T(8,128)}) %all-reduce.11.cloned.1.call-update) | async-done | bytes 5242896 | tf_op jit(solution)/shard_map/psum | solution.py:186
  469.6 5.6 %copy.44 = f32[2560,512]{1,0:T(8,128)} copy(f32[2560,512]{1,0:T(8,128)} %all-reduce.11.cloned.1.call-done) | data formatting | bytes 10485760
  (114 shorter events, 31.5 us)
Async XLA Ops:
  7.2 143.3 %copy-start = (bf16[2560,512]{1,0:T(8,128)(2,1)S(1)}, bf16[2560,512]{1,0:T(8,128)(2,1)}, u32[]{:S(2)}) copy-start(bf16[2560,512]{1,0:T(8,128)(2,1)} %param.9) | copy-start | bytes 7864324
  8.5 15.7 %collective-permute-start.2 = (f32[5,16,2,128]{3,2,1,0:T(2,128)S(1)}, f32[5,16,2,128]{3,2,1,0:T(2,128)}, u32[]{:S(2)}, u32[]{:S(2)}) collective-permute-start(f32[5,16,2,128]{3,2,1,0:T(2,128)S(1)} %get-tuple-element.39), channel_id=1, source_target_pairs={{0,1},{1,2},{2,3},{3,4},{4,5},{5,6},{6,7},{8,9},{9,10},{10,11},{11... | collective-permute-start | bytes 245768 | tf_op jit(solution)/shard_map/ppermute | solution.py:27
  13.1 11.9 %collective-permute-start.3 = (f32[5,16,2,128]{3,2,1,0:T(2,128)S(1)}, f32[5,16,2,128]{3,2,1,0:T(2,128)}, u32[]{:S(2)}, u32[]{:S(2)}) collective-permute-start(f32[5,16,2,128]{3,2,1,0:T(2,128)S(1)} %get-tuple-element.40), channel_id=1, source_target_pairs={{1,0},{2,1},{3,2},{4,3},{5,4},{6,5},{7,6},{9,8},{10,9},{11,10},{12... | collective-permute-start | bytes 245768 | tf_op jit(solution)/shard_map/ppermute | solution.py:28
  15.5 12.4 %collective-permute-start.1 = (f32[5,2,32,128]{3,2,1,0:T(8,128)S(1)}, f32[5,2,32,128]{3,2,1,0:T(8,128)S(1)}, u32[]{:S(2)}, u32[]{:S(2)}) collective-permute-start(f32[5,2,32,128]{3,2,1,0:T(8,128)S(1)} %get-tuple-element.41), channel_id=1, source_target_pairs={{8,0},{16,8},{24,16},{32,24},{40,32},{48,40},{56,48},{64,56},{72,6... | collective-permute-start | bytes 491528 | tf_op jit(solution)/shard_map/ppermute | solution.py:28
  18.3 7.7 %collective-permute-start = (f32[5,2,32,128]{3,2,1,0:T(8,128)S(1)}, f32[5,2,32,128]{3,2,1,0:T(8,128)S(1)}, u32[]{:S(2)}, u32[]{:S(2)}) collective-permute-start(f32[5,2,32,128]{3,2,1,0:T(8,128)S(1)} %get-tuple-element.42), channel_id=1, source_target_pairs={{0,8},{8,16},{16,24},{24,32},{32,40},{40,48},{48,56},{56,64},{64,7... | collective-permute-start | bytes 491528 | tf_op jit(solution)/shard_map/ppermute | solution.py:27
  32.4 1.3 copy-start.6
  33.7 16.1 %copy-start.13 = (s32[64,1]{0,1:T(1,128)S(1)}, s32[64,1]{0,1:T(1,128)}, u32[]{:S(2)}) copy-start(s32[64,1]{0,1:T(1,128)} %param.10) | copy-start | bytes 772
  37.7 1.1 copy-start.4
  38.8 48.7 %collective-permute-start.6 = (f32[5,16,2,128]{3,2,1,0:T(2,128)S(1)}, f32[5,16,2,128]{3,2,1,0:T(2,128)}, u32[]{:S(2)}, u32[]{:S(2)}) collective-permute-start(f32[5,16,2,128]{3,2,1,0:T(2,128)S(1)} %get-tuple-element.34), channel_id=1, source_target_pairs={{0,1},{1,2},{2,3},{3,4},{4,5},{5,6},{6,7},{8,9},{9,10},{10,11},{11... | collective-permute-start | bytes 245768 | tf_op jit(solution)/shard_map/ppermute | solution.py:27
  43.7 44.7 %collective-permute-start.7 = (f32[5,16,2,128]{3,2,1,0:T(2,128)S(1)}, f32[5,16,2,128]{3,2,1,0:T(2,128)}, u32[]{:S(2)}, u32[]{:S(2)}) collective-permute-start(f32[5,16,2,128]{3,2,1,0:T(2,128)S(1)} %get-tuple-element.35), channel_id=1, source_target_pairs={{1,0},{2,1},{3,2},{4,3},{5,4},{6,5},{7,6},{9,8},{10,9},{11,10},{12... | collective-permute-start | bytes 245768 | tf_op jit(solution)/shard_map/ppermute | solution.py:28
  45.0 44.4 %collective-permute-start.4 = (f32[5,2,32,128]{3,2,1,0:T(8,128)S(1)}, f32[5,2,32,128]{3,2,1,0:T(8,128)S(1)}, u32[]{:S(2)}, u32[]{:S(2)}) collective-permute-start(f32[5,2,32,128]{3,2,1,0:T(8,128)S(1)} %get-tuple-element.32), channel_id=1, source_target_pairs={{0,8},{8,16},{16,24},{24,32},{32,40},{40,48},{48,56},{56,64},{64,7... | collective-permute-start | bytes 491528 | tf_op jit(solution)/shard_map/ppermute | solution.py:27
  47.8 41.5 %collective-permute-start.5 = (f32[5,2,32,128]{3,2,1,0:T(8,128)S(1)}, f32[5,2,32,128]{3,2,1,0:T(8,128)S(1)}, u32[]{:S(2)}, u32[]{:S(2)}) collective-permute-start(f32[5,2,32,128]{3,2,1,0:T(8,128)S(1)} %get-tuple-element.33), channel_id=1, source_target_pairs={{8,0},{16,8},{24,16},{32,24},{40,32},{48,40},{56,48},{64,56},{72,6... | collective-permute-start | bytes 491528 | tf_op jit(solution)/shard_map/ppermute | solution.py:28
  94.0 1.3 copy-start.5
  100.5 1.1 copy-start.2
  102.4 57.4 %collective-permute-start.10 = (f32[5,16,2,128]{3,2,1,0:T(2,128)}, f32[5,16,2,128]{3,2,1,0:T(2,128)}, u32[]{:S(2)}, u32[]{:S(2)}) collective-permute-start(f32[5,16,2,128]{3,2,1,0:T(2,128)} %get-tuple-element.30), channel_id=1, source_target_pairs={{0,1},{1,2},{2,3},{3,4},{4,5},{5,6},{6,7},{8,9},{9,10},{10,11},{11... | collective-permute-start | bytes 245768 | tf_op jit(solution)/shard_map/ppermute | solution.py:27
  107.3 53.5 %collective-permute-start.11 = (f32[5,16,2,128]{3,2,1,0:T(2,128)}, f32[5,16,2,128]{3,2,1,0:T(2,128)}, u32[]{:S(2)}, u32[]{:S(2)}) collective-permute-start(f32[5,16,2,128]{3,2,1,0:T(2,128)} %get-tuple-element.31), channel_id=1, source_target_pairs={{1,0},{2,1},{3,2},{4,3},{5,4},{6,5},{7,6},{9,8},{10,9},{11,10},{12... | collective-permute-start | bytes 245768 | tf_op jit(solution)/shard_map/ppermute | solution.py:28
  108.6 53.1 %collective-permute-start.8 = (f32[5,2,32,128]{3,2,1,0:T(8,128)}, f32[5,2,32,128]{3,2,1,0:T(8,128)S(1)}, u32[]{:S(2)}, u32[]{:S(2)}) collective-permute-start(f32[5,2,32,128]{3,2,1,0:T(8,128)} %get-tuple-element.28), channel_id=1, source_target_pairs={{0,8},{8,16},{16,24},{24,32},{32,40},{40,48},{48,56},{56,64},{64,7... | collective-permute-start | bytes 491528 | tf_op jit(solution)/shard_map/ppermute | solution.py:27
  112.5 49.2 %collective-permute-start.9 = (f32[5,2,32,128]{3,2,1,0:T(8,128)}, f32[5,2,32,128]{3,2,1,0:T(8,128)S(1)}, u32[]{:S(2)}, u32[]{:S(2)}) collective-permute-start(f32[5,2,32,128]{3,2,1,0:T(8,128)} %get-tuple-element.29), channel_id=1, source_target_pairs={{8,0},{16,8},{24,16},{32,24},{40,32},{48,40},{56,48},{64,56},{72,6... | collective-permute-start | bytes 491528 | tf_op jit(solution)/shard_map/ppermute | solution.py:28
  166.3 1.3 copy-start.3
  209.0 3.2 copy-start.9
  214.0 40.3 %all-to-all-start = ((bf16[128,2,2049]{2,1,0:T(2,128)(2,1)}), bf16[128,2,2049]{2,1,0:T(2,128)(2,1)S(1)}, u32[]{:S(2)}, u32[]{:S(2)}) async-start(bf16[128,2,2049]{2,1,0:T(2,128)(2,1)} %pad_maximum_fusion.8), calls=%async_computation | async-start | bytes 2228224 | tf_op jit(solution)/shard_map/all_to_all | solution.py:43
  257.8 3.1 copy-start.12
  257.8 3.1 copy-start.14
  257.8 3.1 copy-start.15
  257.8 3.1 copy-start.16
  260.8 2.0 copy-start.7
  262.9 4.4 copy-start.10
  265.9 1.4 copy-start.11
  269.5 38.0 %all-to-all-start.1 = ((bf16[128,2,2,512]{3,2,1,0:T(2,128)(2,1)}), bf16[128,2,2,512]{3,2,1,0:T(2,128)(2,1)S(1)}, u32[]{:S(2)}, u32[]{:S(2)}) async-start(bf16[128,2,2,512]{3,2,1,0:T(2,128)(2,1)} %reshape.81), calls=%async_computation.1 | async-start | bytes 1048576 | tf_op jit(solution)/shard_map/all_to_all | solution.py:177
  274.6 195.1 %all-reduce.11.cloned.1.call-start = ((), (), s32[]{:S(2)}) async-start(), calls=%async_computation.2 | async-start | bytes 10485760 | tf_op jit(solution)/shard_map/psum | solution.py:186
  311.7 5.0 %copy-start.8 = (f32[512,2048]{1,0:T(8,128)S(1)}, f32[512,2048]{1,0:T(8,128)}, u32[]{:S(2)}) copy-start(f32[512,2048]{1,0:T(8,128)} %copy-done.7) | copy-start | bytes 12582916
  469.6 5.6 %copy-start.1 = (bf16[2560,512]{1,0:T(8,128)(2,1)S(1)}, bf16[2560,512]{1,0:T(8,128)(2,1)}, u32[]{:S(2)}) copy-start(bf16[2560,512]{1,0:T(8,128)(2,1)} %param.9) | copy-start | bytes 7864324
Sparse Core Ops, SparseCore 0:
  311.8 157.7 all-reduce.10
where the time goes:
time: 491 us; the launch traced here: 482 us
  waiting for transfers between devices  169 us (34%)
  local copies, waits for them, and re-layouts  166 us (34%)
  starting transfers between devices  60.9 us (12%)
  other arithmetic  47.8 us (10%)
  matrix products  23.2 us (5%)
  between operations  15.2 us (3%)
    psum x1, waiting for transfers between devices, per_device(): patch_gradient = lax.psum(partial_value, ('gx', 'gy'))  149 us
    reshape x3, local copies, waits for them, and re-layouts, patchify(): state.reshape(FIELDS, width_x // PATCH, PATCH, width_y // PATCH, PATCH, w...  43.3 us
    transpose x3, local copies, waits for them, and re-layouts, patchify(): shaped.transpose(1, 3, 5, 0, 2, 4, 6).reshape(-1, FIELDS * PATCH ** 3)  40 us
    ppermute x6, starting transfers between devices, with_halo(): lax.ppermute(last, axis, up)  24.7 us
    reshape x3, local copies, waits for them, and re-layouts, patchify(): shaped.transpose(1, 3, 5, 0, 2, 4, 6).reshape(-1, FIELDS * PATCH ** 3)  23.7 us
    select_n x2, local copies, waits for them, and re-layouts, per_device(): jnp.where(lag_rows == 1, patchify(states[1].astype(jnp.bfloat16)), picked)  20.7 us
    all_to_all x1, starting transfers between devices, sent_together(): lax.all_to_all(both, axis, split_axis=split_dim, concat_axis=concat_dim,...  20.5 us
    all_to_all x1, waiting for transfers between devices, sent_together(): lax.all_to_all(both, axis, split_axis=split_dim, concat_axis=concat_dim,...  19.8 us
  transfers between devices with their start and end apart: 15, of which 2 were waited for; matrix products, arithmetic and copies ran while one was open for 28% of the time, Pallas kernels for 0%

commit v1 on v0

--- a/solution.py
+++ b/solution.py
@@ -183,7 +183,7 @@
     )
     source_grad = returned.reshape(devices * slot_count, BLOCK_ROWS, EMBED)[block_slot]
     partial_value = contract_rows(picked, source_grad.reshape(patch_count, EMBED))
-    patch_gradient = lax.psum(partial_value, ("gx", "gy"))
+    patch_gradient = lax.psum(lax.psum(partial_value, "gy"), "gx")
     return (
         states[-1],
         patch_gradient,

time: 491 us -> 599 us (1.22)
  waiting for transfers between devices: 169 us -> 277 us
    psum x1 -> x2, waiting for transfers between devices: 149 us -> 257 us  [per_device(): patch_gradient = lax.psum(lax.psum(partial_value, 'gy'), 'gx')]
  transfers between devices with their start and end apart: 15 -> 16, of which waited for: 2 -> 3; matrix products, arithmetic and copies ran while one was open for 28% -> 23% of each run, Pallas kernels for 0% -> 0%
where the time goes in v1:
time: 599 us; the launch traced here: 590 us
  waiting for transfers between devices  277 us (46%)
  local copies, waits for them, and re-layouts  166 us (28%)
  starting transfers between devices  61 us (10%)
  other arithmetic  47.8 us (8%)
  matrix products  23.2 us (4%)
  between operations  15.2 us (3%)
    psum x2, waiting for transfers between devices, per_device(): patch_gradient = lax.psum(lax.psum(partial_value, 'gy'), 'gx')  257 us
    reshape x3, local copies, waits for them, and re-layouts, patchify(): state.reshape(FIELDS, width_x // PATCH, PATCH, width_y // PATCH, PATCH, w...  43.3 us
    transpose x3, local copies, waits for them, and re-layouts, patchify(): shaped.transpose(1, 3, 5, 0, 2, 4, 6).reshape(-1, FIELDS * PATCH ** 3)  40 us
    ppermute x6, starting transfers between devices, with_halo(): lax.ppermute(last, axis, up)  24.7 us
    reshape x3, local copies, waits for them, and re-layouts, patchify(): shaped.transpose(1, 3, 5, 0, 2, 4, 6).reshape(-1, FIELDS * PATCH ** 3)  23.7 us
    select_n x2, local copies, waits for them, and re-layouts, per_device(): jnp.where(lag_rows == 1, patchify(states[1].astype(jnp.bfloat16)), picked)  20.7 us
    all_to_all x1, starting transfers between devices, sent_together(): lax.all_to_all(both, axis, split_axis=split_dim, concat_axis=concat_dim,...  20.5 us
    all_to_all x1, waiting for transfers between devices, sent_together(): lax.all_to_all(both, axis, split_axis=split_dim, concat_axis=concat_dim,...  19.8 us
  transfers between devices with their start and end apart: 16, of which 3 were waited for; matrix products, arithmetic and copies ran while one was open for 23% of the time, Pallas kernels for 0%

profile of v1, /device:TPU:1, one launch (start us, length us, event | category | flops | bytes accessed | tf_op | source)
XLA Modules:
  0.0 590.4 jit_solution(1267329495844191305)
XLA Ops:
  8.5 4.7 collective-permute-start.2
  15.5 2.9 collective-permute-start.1
  18.3 3.4 collective-permute-start
  26.1 1.8 constant_dynamic-update-slice_fusion
  27.9 1.6 select_maximum_fusion.8
  29.5 2.3 broadcast_multiply_fusion.2
  33.7 4.0 fusion.57
  38.8 4.9 collective-permute-start.6
  45.0 2.8 collective-permute-start.4
  47.8 1.9 collective-permute-start.5
  49.9 1.5 scatter_custom_fusion.2
  51.6 14.5 %reshape.74 = bf16[5,2,8,4,8,16,8]{6,5,4,3,2,1,0:T(8,128)(2,1)} reshape(bf16[5,16,32,128]{3,2,1,0:T(8,128)(2,1)} %get-tuple-element.10) | data formatting | bytes 1310720 | tf_op jit(solution)/shard_map/reshape | solution.py:114
  66.1 13.3 %copy.21 = bf16[2,4,16,5,8,8,8]{2,1,0,6,5,4,3:T(4,128)(2,1)} copy(bf16[2,4,16,5,8,8,8]{6,2,5,1,4,0,3:T(8,128)(2,1)} %bitcast.73) | data formatting | bytes 1310720 | tf_op jit(solution)/shard_map/transpose | solution.py:117
  79.4 8.1 %reshape.76 = bf16[128,2560]{0,1:T(8,128)(2,1)} reshape(bf16[2,4,16,5,8,8,8]{2,1,0,6,5,4,3:T(4,128)(2,1)} %copy.21) | data formatting | bytes 1310720 | tf_op jit(solution)/shard_map/reshape | solution.py:117
  89.4 4.6 select_maximum_fusion.4
  96.7 3.9 fusion.55
  102.4 4.9 collective-permute-start.10
  108.6 3.9 collective-permute-start.8
  112.5 2.1 collective-permute-start.9
  114.6 14.4 %reshape.73 = bf16[5,2,8,4,8,16,8]{6,5,4,3,2,1,0:T(8,128)(2,1)} reshape(bf16[5,16,32,128]{3,2,1,0:T(8,128)(2,1)} %get-tuple-element.8) | data formatting | bytes 1310720 | tf_op jit(solution)/shard_map/reshape | solution.py:114
  129.1 13.3 %copy.20 = bf16[2,4,16,5,8,8,8]{2,1,0,6,5,4,3:T(4,128)(2,1)} copy(bf16[2,4,16,5,8,8,8]{6,2,5,1,4,0,3:T(8,128)(2,1)} %bitcast.74) | data formatting | bytes 1310720 | tf_op jit(solution)/shard_map/transpose | solution.py:117
  142.4 8.1 %reshape.75 = bf16[128,2560]{0,1:T(8,128)(2,1)} reshape(bf16[2,4,16,5,8,8,8]{2,1,0,6,5,4,3:T(4,128)(2,1)} %copy.20) | data formatting | bytes 1310720 | tf_op jit(solution)/shard_map/reshape | solution.py:117
  150.5 1.8 convolution_convert_fusion.1
  153.3 5.4 scatter_fusion
  161.7 4.6 select_maximum_fusion
  169.0 4.1 fusion.53
  173.1 14.4 %reshape.78 = bf16[5,2,8,4,8,16,8]{6,5,4,3,2,1,0:T(8,128)(2,1)} reshape(bf16[5,16,32,128]{3,2,1,0:T(8,128)(2,1)} %get-tuple-element.6) | data formatting | bytes 1310720 | tf_op jit(solution)/shard_map/reshape | solution.py:114
  187.6 13.3 %copy.22 = bf16[2,4,16,5,8,8,8]{2,1,0,6,5,4,3:T(4,128)(2,1)} copy(bf16[2,4,16,5,8,8,8]{6,2,5,1,4,0,3:T(8,128)(2,1)} %bitcast.75) | data formatting | bytes 1310720 | tf_op jit(solution)/shard_map/transpose | solution.py:117
  200.9 7.5 %reshape.79 = bf16[128,2560]{0,1:T(8,128)(2,1)S(1)} reshape(bf16[2,4,16,5,8,8,8]{2,1,0,6,5,4,3:T(4,128)(2,1)} %copy.22) | data formatting | bytes 1310720 | tf_op jit(solution)/shard_map/reshape | solution.py:117
  209.3 2.5 scatter_fusion.1
  212.2 1.9 pad_maximum_fusion.8
  214.0 20.5 %all-to-all-start = ((bf16[128,2,2049]{2,1,0:T(2,128)(2,1)}), bf16[128,2,2049]{2,1,0:T(2,128)(2,1)S(1)}, u32[]{:S(2)}, u32[]{:S(2)}) async-start(bf16[128,2,2049]{2,1,0:T(2,128)(2,1)} %pad_maximum_fusion.8), calls=%async_computation | async-start | bytes 2228224 | tf_op jit(solution)/shard_map/all_to_all | solution.py:43
  234.5 19.8 %all-to-all-done = bf16[128,2,2049]{2,1,0:T(2,128)(2,1)S(1)} async-done(((bf16[128,2,2049]{2,1,0:T(2,128)(2,1)}), bf16[128,2,2049]{2,1,0:T(2,128)(2,1)S(1)}, u32[]{:S(2)}, u32[]{:S(2)}) %all-to-all-start) | async-done | bytes 1049120 | tf_op jit(solution)/shard_map/all_to_all | solution.py:43
  255.6 1.8 reshape.84
  257.8 3.0 fusion.6
  260.9 1.9 convert_reduce_fusion.1
  262.9 3.0 convert_reduce_fusion
  265.9 1.4 copy-done.11
  269.5 5.0 all-to-all-start.1
  274.6 12.3 %broadcast_select_fusion = bf16[2,4,16,5,8,8,8]{6,2,5,1,4,0,3:T(8,128)(2,1)} fusion(pred[2,4,16]{2,1,0:T(4,128)(4,1)S(1)} %broadcast_compare_fusion, bf16[5,2,8,4,8,16,8]{6,5,4,3,2,1,0:T(8,128)(2,1)} %reshape.74, bf16[5,2,8,4,8,16,8]{6,5,4,3,2,1,0:T(8,128)(2,1)} %reshape.73), kind=kLoop, calls=%fused_computation.4 | loop fusion | flops 327680 | bytes 1966208 | tf_op jit(solution)/shard_map/jit(_where)/select_n | solution.py:139
  286.9 13.3 %copy.19 = bf16[2,4,16,5,8,8,8]{2,1,0,6,5,4,3:T(4,128)(2,1)} copy(bf16[2,4,16,5,8,8,8]{6,2,5,1,4,0,3:T(8,128)(2,1)} %broadcast_select_fusion) | data formatting | bytes 1310720 | tf_op jit(solution)/shard_map/jit(_where)/select_n | solution.py:139
  300.2 7.3 %select_n.17 = bf16[128,2560]{0,1:T(8,128)(2,1)S(1)} reshape(bf16[2,4,16,5,8,8,8]{2,1,0,6,5,4,3:T(4,128)(2,1)} %copy.19) | data formatting | bytes 1310720 | tf_op jit(solution)/shard_map/jit(_where)/select_n | solution.py:139
  308.5 3.2 fusion.65
  311.7 128.6 %all-reduce.12.cloned.1.call-done = f32[2560,512]{1,0:T(8,128)} async-done(((f32[2560,512]{1,0:T(8,128)}), f32[2560,512]{1,0:T(8,128)}) %all-reduce.12.cloned.1.call-update) | async-done | bytes 5242896 | tf_op jit(solution)/shard_map/psum | solution.py:186
  440.3 5.0 convolution_bitcast_fusion.1
  445.4 3.5 convolution_bitcast_fusion
  448.8 128.7 %all-reduce.14.cloned.1.call-done = f32[2560,512]{1,0:T(8,128)} async-done(((f32[2560,512]{1,0:T(8,128)}), f32[2560,512]{1,0:T(8,128)}) %all-reduce.14.cloned.1.call-update) | async-done | bytes 5242896 | tf_op jit(solution)/shard_map/psum | solution.py:186
  577.5 5.6 copy.45
  (117 shorter events, 32.8 us)
Async XLA Ops:
  7.2 143.3 %copy-start = (bf16[2560,512]{1,0:T(8,128)(2,1)S(1)}, bf16[2560,512]{1,0:T(8,128)(2,1)}, u32[]{:S(2)}) copy-start(bf16[2560,512]{1,0:T(8,128)(2,1)} %param.9) | copy-start | bytes 7864324
  8.5 15.7 %collective-permute-start.2 = (f32[5,16,2,128]{3,2,1,0:T(2,128)S(1)}, f32[5,16,2,128]{3,2,1,0:T(2,128)}, u32[]{:S(2)}, u32[]{:S(2)}) collective-permute-start(f32[5,16,2,128]{3,2,1,0:T(2,128)S(1)} %get-tuple-element.39), channel_id=1, source_target_pairs={{0,1},{1,2},{2,3},{3,4},{4,5},{5,6},{6,7},{8,9},{9,10},{10,11},{11... | collective-permute-start | bytes 245768 | tf_op jit(solution)/shard_map/ppermute | solution.py:27
  13.1 11.9 %collective-permute-start.3 = (f32[5,16,2,128]{3,2,1,0:T(2,128)S(1)}, f32[5,16,2,128]{3,2,1,0:T(2,128)}, u32[]{:S(2)}, u32[]{:S(2)}) collective-permute-start(f32[5,16,2,128]{3,2,1,0:T(2,128)S(1)} %get-tuple-element.40), channel_id=1, source_target_pairs={{1,0},{2,1},{3,2},{4,3},{5,4},{6,5},{7,6},{9,8},{10,9},{11,10},{12... | collective-permute-start | bytes 245768 | tf_op jit(solution)/shard_map/ppermute | solution.py:28
  15.5 12.4 %collective-permute-start.1 = (f32[5,2,32,128]{3,2,1,0:T(8,128)S(1)}, f32[5,2,32,128]{3,2,1,0:T(8,128)S(1)}, u32[]{:S(2)}, u32[]{:S(2)}) collective-permute-start(f32[5,2,32,128]{3,2,1,0:T(8,128)S(1)} %get-tuple-element.41), channel_id=1, source_target_pairs={{8,0},{16,8},{24,16},{32,24},{40,32},{48,40},{56,48},{64,56},{72,6... | collective-permute-start | bytes 491528 | tf_op jit(solution)/shard_map/ppermute | solution.py:28
  18.3 7.7 %collective-permute-start = (f32[5,2,32,128]{3,2,1,0:T(8,128)S(1)}, f32[5,2,32,128]{3,2,1,0:T(8,128)S(1)}, u32[]{:S(2)}, u32[]{:S(2)}) collective-permute-start(f32[5,2,32,128]{3,2,1,0:T(8,128)S(1)} %get-tuple-element.42), channel_id=1, source_target_pairs={{0,8},{8,16},{16,24},{24,32},{32,40},{40,48},{48,56},{56,64},{64,7... | collective-permute-start | bytes 491528 | tf_op jit(solution)/shard_map/ppermute | solution.py:27
  32.4 1.3 copy-start.6
  33.7 16.1 %copy-start.13 = (s32[64,1]{0,1:T(1,128)S(1)}, s32[64,1]{0,1:T(1,128)}, u32[]{:S(2)}) copy-start(s32[64,1]{0,1:T(1,128)} %param.10) | copy-start | bytes 772
  37.7 1.1 copy-start.4
  38.8 48.7 %collective-permute-start.6 = (f32[5,16,2,128]{3,2,1,0:T(2,128)S(1)}, f32[5,16,2,128]{3,2,1,0:T(2,128)}, u32[]{:S(2)}, u32[]{:S(2)}) collective-permute-start(f32[5,16,2,128]{3,2,1,0:T(2,128)S(1)} %get-tuple-element.34), channel_id=1, source_target_pairs={{0,1},{1,2},{2,3},{3,4},{4,5},{5,6},{6,7},{8,9},{9,10},{10,11},{11... | collective-permute-start | bytes 245768 | tf_op jit(solution)/shard_map/ppermute | solution.py:27
  43.7 44.7 %collective-permute-start.7 = (f32[5,16,2,128]{3,2,1,0:T(2,128)S(1)}, f32[5,16,2,128]{3,2,1,0:T(2,128)}, u32[]{:S(2)}, u32[]{:S(2)}) collective-permute-start(f32[5,16,2,128]{3,2,1,0:T(2,128)S(1)} %get-tuple-element.35), channel_id=1, source_target_pairs={{1,0},{2,1},{3,2},{4,3},{5,4},{6,5},{7,6},{9,8},{10,9},{11,10},{12... | collective-permute-start | bytes 245768 | tf_op jit(solution)/shard_map/ppermute | solution.py:28
  45.0 44.4 %collective-permute-start.4 = (f32[5,2,32,128]{3,2,1,0:T(8,128)S(1)}, f32[5,2,32,128]{3,2,1,0:T(8,128)S(1)}, u32[]{:S(2)}, u32[]{:S(2)}) collective-permute-start(f32[5,2,32,128]{3,2,1,0:T(8,128)S(1)} %get-tuple-element.32), channel_id=1, source_target_pairs={{0,8},{8,16},{16,24},{24,32},{32,40},{40,48},{48,56},{56,64},{64,7... | collective-permute-start | bytes 491528 | tf_op jit(solution)/shard_map/ppermute | solution.py:27
  47.8 41.5 %collective-permute-start.5 = (f32[5,2,32,128]{3,2,1,0:T(8,128)S(1)}, f32[5,2,32,128]{3,2,1,0:T(8,128)S(1)}, u32[]{:S(2)}, u32[]{:S(2)}) collective-permute-start(f32[5,2,32,128]{3,2,1,0:T(8,128)S(1)} %get-tuple-element.33), channel_id=1, source_target_pairs={{8,0},{16,8},{24,16},{32,24},{40,32},{48,40},{56,48},{64,56},{72,6... | collective-permute-start | bytes 491528 | tf_op jit(solution)/shard_map/ppermute | solution.py:28
  94.0 1.3 copy-start.5
  100.5 1.1 copy-start.2
  102.4 57.4 %collective-permute-start.10 = (f32[5,16,2,128]{3,2,1,0:T(2,128)}, f32[5,16,2,128]{3,2,1,0:T(2,128)}, u32[]{:S(2)}, u32[]{:S(2)}) collective-permute-start(f32[5,16,2,128]{3,2,1,0:T(2,128)} %get-tuple-element.30), channel_id=1, source_target_pairs={{0,1},{1,2},{2,3},{3,4},{4,5},{5,6},{6,7},{8,9},{9,10},{10,11},{11... | collective-permute-start | bytes 245768 | tf_op jit(solution)/shard_map/ppermute | solution.py:27
  107.3 53.5 %collective-permute-start.11 = (f32[5,16,2,128]{3,2,1,0:T(2,128)}, f32[5,16,2,128]{3,2,1,0:T(2,128)}, u32[]{:S(2)}, u32[]{:S(2)}) collective-permute-start(f32[5,16,2,128]{3,2,1,0:T(2,128)} %get-tuple-element.31), channel_id=1, source_target_pairs={{1,0},{2,1},{3,2},{4,3},{5,4},{6,5},{7,6},{9,8},{10,9},{11,10},{12... | collective-permute-start | bytes 245768 | tf_op jit(solution)/shard_map/ppermute | solution.py:28
  108.6 53.1 %collective-permute-start.8 = (f32[5,2,32,128]{3,2,1,0:T(8,128)}, f32[5,2,32,128]{3,2,1,0:T(8,128)S(1)}, u32[]{:S(2)}, u32[]{:S(2)}) collective-permute-start(f32[5,2,32,128]{3,2,1,0:T(8,128)} %get-tuple-element.28), channel_id=1, source_target_pairs={{0,8},{8,16},{16,24},{24,32},{32,40},{40,48},{48,56},{56,64},{64,7... | collective-permute-start | bytes 491528 | tf_op jit(solution)/shard_map/ppermute | solution.py:27
  112.5 49.2 %collective-permute-start.9 = (f32[5,2,32,128]{3,2,1,0:T(8,128)}, f32[5,2,32,128]{3,2,1,0:T(8,128)S(1)}, u32[]{:S(2)}, u32[]{:S(2)}) collective-permute-start(f32[5,2,32,128]{3,2,1,0:T(8,128)} %get-tuple-element.29), channel_id=1, source_target_pairs={{8,0},{16,8},{24,16},{32,24},{40,32},{48,40},{56,48},{64,56},{72,6... | collective-permute-start | bytes 491528 | tf_op jit(solution)/shard_map/ppermute | solution.py:28
  166.3 1.3 copy-start.3
  209.0 3.2 copy-start.9
  214.0 40.3 %all-to-all-start = ((bf16[128,2,2049]{2,1,0:T(2,128)(2,1)}), bf16[128,2,2049]{2,1,0:T(2,128)(2,1)S(1)}, u32[]{:S(2)}, u32[]{:S(2)}) async-start(bf16[128,2,2049]{2,1,0:T(2,128)(2,1)} %pad_maximum_fusion.8), calls=%async_computation | async-start | bytes 2228224 | tf_op jit(solution)/shard_map/all_to_all | solution.py:43
  257.8 3.1 copy-start.12
  257.8 3.1 copy-start.14
  257.8 3.1 copy-start.15
  257.8 3.1 copy-start.16
  260.8 2.0 copy-start.7
  262.9 4.4 copy-start.10
  265.9 1.4 copy-start.11
  269.5 38.0 %all-to-all-start.1 = ((bf16[128,2,2,512]{3,2,1,0:T(2,128)(2,1)}), bf16[128,2,2,512]{3,2,1,0:T(2,128)(2,1)S(1)}, u32[]{:S(2)}, u32[]{:S(2)}) async-start(bf16[128,2,2,512]{3,2,1,0:T(2,128)(2,1)} %reshape.81), calls=%async_computation.1 | async-start | bytes 1048576 | tf_op jit(solution)/shard_map/all_to_all | solution.py:177
  274.6 165.7 %all-reduce.12.cloned.1.call-start = ((), (), s32[]{:S(2)}) async-start(), calls=%async_computation.2 | async-start | bytes 10485760 | tf_op jit(solution)/shard_map/psum | solution.py:186
  311.7 265.9 %all-reduce.14.cloned.1.call-start = ((), (), s32[]{:S(2)}) async-start(), calls=%async_computation.3 | async-start | bytes 10485760 | tf_op jit(solution)/shard_map/psum | solution.py:186
  440.3 5.0 copy-start.8
  577.5 5.6 copy-start.1
Sparse Core Ops, SparseCore 0:
  311.8 128.4 all-reduce.11
  442.8 134.6 all-reduce.13
